TPU v7x, 128 devices: a whole 4x4x4 slice. The times are simulated.
128 devices in a mesh: row: 8 (over y, core), col: 16 (over x, z).
Axes of the slice: x: 4, y: 4, z: 4, core: 2. Of those that a mesh axis runs over, the one named last changes fastest.
Arguments:
- ancestor: bfloat16 [128, 128, 256, 256], P('row', 'col'), may hold values from -6 to 6
- tile_mask: int32 [128, 128], P('row', 'col'), may hold values 0 or 1
- member_one: int32 [128], replicated, may hold values 0 or 1
- member_two: int32 [128], replicated, may hold values 0 or 1
- factor_one: bfloat16 [128, 256, 256], P('row'), may hold values from -0.03125 to 0.03125
- factor_two: bfloat16 [128, 256, 256], P('row'), may hold values from -0.03125 to 0.03125
- link_block: bfloat16 [256, 256], replicated, may hold values from -0.375 to 0.375
- inverse_one: float32 [256, 256], replicated, may hold values from -6 to 6
- inverse_two: float32 [256, 256], replicated, may hold values from -6 to 6
Outputs:
- column_one: bfloat16 [128, 256, 256], P(('row', 'col'))
- column_two: bfloat16 [128, 256, 256], P(('row', 'col'))
- diag_one: bfloat16 [256, 256], replicated
- cross_block: bfloat16 [256, 256], replicated
- diag_two: bfloat16 [256, 256], replicated
All inputs are finite; a program needn't handle non-finite values. No bound on the sum of `tile_mask` on one device may be relied on, other than what follows from the above.
Results may differ from a plain program's by a relative error of at most 0.01.
Values may be sent and summed in bfloat16 or wider, within the bound.
A program may use at most 128 MiB of HBM per device.

v0:
```python
import jax
import jax.numpy as jnp
from jax import lax
from jax.sharding import PartitionSpec as P


def from_root(block, axis, owner):
    block = jnp.where(lax.axis_index(axis) == owner, block, jnp.zeros_like(block))
    return lax.psum(block, axis)


def shards(
    ancestor,
    tile_mask,
    member_one,
    member_two,
    factor_one,
    factor_two,
    link_block,
    inverse_one,
    inverse_two,
):
    hp = lax.Precision.HIGHEST
    rows_count = lax.axis_size("row")
    cols_count = lax.axis_size("col")
    row_index = lax.axis_index("row")
    col_index = lax.axis_index("col")
    rows_local = ancestor.shape[0]
    cols_local = ancestor.shape[1]
    zero = jnp.zeros((), jnp.bfloat16)
    first_start = row_index * rows_local
    flags_one = lax.dynamic_slice_in_dim(member_one, first_start, rows_local, 0)
    flags_two = lax.dynamic_slice_in_dim(member_two, first_start, rows_local, 0)
    first = jnp.where(flags_one[:, None, None] > 0, factor_one, zero)
    second = jnp.where(flags_two[:, None, None] > 0, factor_two, zero)
    group_size = cols_count // rows_count
    owner_row = col_index // group_size
    offset = col_index % group_size * cols_local
    piece_one = lax.dynamic_slice_in_dim(first, offset, cols_local, 0)
    piece_two = lax.dynamic_slice_in_dim(second, offset, cols_local, 0)
    column_first, column_second = (
        from_root(piece_one, "row", owner_row),
        from_root(piece_two, "row", owner_row),
    )
    column_both = jnp.stack([column_first, column_second], 1)
    kept = jnp.where(tile_mask[:, :, None, None] > 0, ancestor, zero)
    reduced = lax.psum_scatter(
        jnp.einsum("ijab,jkbc->ikac", kept, column_both, preferred_element_type=jnp.float32),
        "col",
        scatter_dimension=0,
        tiled=True,
    )
    own_slot = row_index * cols_count + col_index
    weight_one = lax.dynamic_slice_in_dim(member_one, own_slot, 1, 0).astype(jnp.float32)[
        :, None, None
    ]
    weight_two = lax.dynamic_slice_in_dim(member_two, own_slot, 1, 0).astype(jnp.float32)[
        :, None, None
    ]
    rows_first = lax.dynamic_slice_in_dim(first, col_index, 1, 0)
    rows_second = lax.dynamic_slice_in_dim(second, col_index, 1, 0)
    y_one = weight_one * reduced[:, 0]
    column_one = (-y_one).astype(jnp.bfloat16)
    y_two = weight_two * (
        reduced[:, 1]
        + jnp.einsum("sab,bc->sac", column_one, link_block, preferred_element_type=jnp.float32)
    )
    column_two = (-y_two).astype(jnp.bfloat16)
    v_part = jnp.einsum("sab,sac->bc", column_one, rows_second, preferred_element_type=jnp.float32)
    part_one = jnp.einsum("sab,sac->bc", rows_first.astype(jnp.float32), y_one, precision=hp)
    part_two = jnp.einsum("sab,sac->bc", rows_second.astype(jnp.float32), y_two, precision=hp)
    sum_one, vsum, carried = lax.psum((part_one, v_part, part_two), ("row", "col"))
    diag_one = (inverse_one + sum_one).astype(jnp.bfloat16)
    cross_block = (
        -(vsum + jnp.dot(diag_one, link_block, preferred_element_type=jnp.float32))
    ).astype(jnp.bfloat16)
    diag_two = (
        inverse_two
        + carried
        - jnp.dot(link_block.T, cross_block, preferred_element_type=jnp.float32)
    ).astype(jnp.bfloat16)
    return (column_one, column_two, diag_one, cross_block, diag_two)


def solution(mesh):
    in_specs = (
        P("row", "col", None, None),
        P("row", "col"),
        P(),
        P(),
        P("row", None, None),
        P("row", None, None),
        P(),
        P(),
        P(),
    )
    out_specs = (P(("row", "col"), None, None), P(("row", "col"), None, None), P(), P(), P())
    return jax.shard_map(shards, mesh=mesh, in_specs=in_specs, out_specs=out_specs, check_vma=False)
```

profile of v0, /device:TPU:1, one launch (start us, length us, event | category | flops | bytes accessed | tf_op | source)
XLA Modules:
  0.0 412.6 jit_solution(11337005895664618917)
XLA Ops:
  7.3 3.9 copy.21
  11.2 2.9 copy.22
  14.2 1.8 broadcast_select_fusion.1
  16.2 1.1 copy-done.2
  17.3 1.2 select_bitcast_fusion.1
  18.5 0.6 copy-done.1
  19.1 1.0 select_bitcast_fusion
  20.3 67.1 %all-reduce.11.cloned.1.call-done = (bf16[8,1,256,256]{2,3,0,1:T(8,128)(2,1)}, bf16[8,1,256,256]{2,3,0,1:T(8,128)(2,1)}) async-done(((bf16[8,1,256,256]{2,3,0,1:T(8,128)(2,1)}, bf16[8,1,256,256]{2,3,0,1:T(8,128)(2,1)}), (bf16[8,1,256,256]{2,3,0,1:T(8,128)(2,1)}, bf16[8,1,256,256]{2,3,0,1:T(8,128)(2,1)})) %all-reduce.11.cloned.1.call-update) | async-done | bytes 2097168 | tf_op jit(solution)/shard_map/psum | solution.py:9
  87.4 15.1 %fusion.5 = f32[16,2,256,256]{2,3,0,1:T(8,128)} fusion(bf16[16,8,256,256]{3,2,1,0:T(8,128)(2,1)} %param.9, pred[16,8]{1,0:T(8,128)(4,1)S(1)} %copy.23, bf16[8,1,256,256]{2,3,0,1:T(8,128)(2,1)} %get-tuple-element.18, bf16[8,1,256,256]{2,3,0,1:T(8,128)(2,1)} %get-tuple-element.19), kind=kOutput, calls=%fused_computation.5 | convolution fusion | flops 8602517504 | bytes 27263104 | tf_op jit(solution)/shard_map/ijab,jkbc->ikac/dot_general | solution.py:48
  102.6 0.6 dynamic_slice.24
  103.1 0.6 dynamic_slice.29
  105.0 0.6 dynamic-slice
  105.6 139.7 %all-reduce.7.cloned.1.call-done = f32[16,2,256,256]{2,3,0,1:T(8,128)} async-done(((f32[16,2,256,256]{2,3,0,1:T(8,128)}), f32[16,2,256,256]{2,3,0,1:T(8,128)}) %all-reduce.7.cloned.1.call-update) | async-done | bytes 8388624
  245.3 1.7 constant_dynamic-slice_fusion
  247.2 1.9 fusion.20
  249.1 0.2 fusion.11
  249.3 2.0 fusion.18
  251.3 2.7 fusion.15
  254.0 0.8 copy.26
  254.8 0.7 fusion.17
  255.5 146.4 %all-reduce.9.cloned.1.call-done = (f32[256,256]{1,0:T(8,128)}, f32[256,256]{1,0:T(8,128)}, f32[256,256]{1,0:T(8,128)}) async-done(((f32[256,256]{1,0:T(8,128)}, f32[256,256]{1,0:T(8,128)}, f32[256,256]{1,0:T(8,128)}), (f32[256,256]{1,0:T(8,128)}, f32[256,256]{1,0:T(8,128)}, f32[256,256]{1,0:T(8,128)})) %all-reduce.9.cloned.1.call-update) | async-done | bytes 786448 | tf_op jit(solution)/shard_map/psum | solution.py:72
  401.9 1.0 add_convert_fusion
  402.9 1.2 fusion.14
  404.1 1.9 fusion.13
  (31 shorter events, 0.7 us)
Async XLA Ops:
  7.2 241.9 %copy-start = (bf16[256,256]{1,0:T(8,128)(2,1)S(1)}, bf16[256,256]{1,0:T(8,128)(2,1)}, u32[]{:S(2)}) copy-start(bf16[256,256]{1,0:T(8,128)(2,1)} %param.15) | copy-start | bytes 393220
  7.2 80.2 %all-reduce.11.cloned.1.call-start = ((), (), s32[]{:S(2)}) async-start(), calls=%async_computation.2 | async-start | bytes 4194304 | tf_op jit(solution)/shard_map/psum | solution.py:9
  11.2 2.9 copy-start.8
  11.2 2.9 copy-start.9
  16.0 1.3 copy-start.2
  17.3 1.7 copy-start.1
  19.1 1.1 copy-start.7
  20.1 225.2 %all-reduce.7.cloned.1.call-start = ((), (), s32[]{:S(2)}) async-start(), calls=%async_computation | async-start | bytes 16777216
  102.5 2.6 copy-start.10
  102.5 299.4 %all-reduce.9.cloned.1.call-start = ((), (), s32[]{:S(2)}) async-start(), calls=%async_computation.1 | async-start | bytes 1572864 | tf_op jit(solution)/shard_map/psum | solution.py:72
  247.2 154.7 %copy-start.6 = (f32[256,256]{1,0:T(8,128)S(1)}, f32[256,256]{1,0:T(8,128)}, u32[]{:S(2)}) copy-start(f32[256,256]{1,0:T(8,128)} %param.16) | copy-start | bytes 786436
  249.3 154.8 %copy-start.5 = (f32[256,256]{1,0:T(8,128)S(1)}, f32[256,256]{1,0:T(8,128)}, u32[]{:S(2)}) copy-start(f32[256,256]{1,0:T(8,128)} %param.17) | copy-start | bytes 786436
  402.9 3.1 copy-start.3
  404.1 1.9 copy-start.4
Sparse Core Ops, SparseCore 0:
  20.3 67.0 all-reduce.10
  102.6 142.6 all-reduce.6
  254.2 147.7 all-reduce.8
where the time goes:
time: 413 us
  waiting for transfers between devices  353 us (85%)
  matrix products  24.9 us (6%)
  between operations  15.3 us (4%)
  local copies, waits for them, and re-layouts  11.3 us (3%)
  other arithmetic  7.64 us (2%)
    psum x1, waiting for transfers between devices, shards(): lax.psum((part_one, v_part, part_two), ('row', 'col'))  146 us
    unnamed x4, waiting for transfers between devices  140 us
    psum x1, waiting for transfers between devices, from_root(): return lax.psum(block, axis)  67.1 us
    dot_general x1, matrix products, shards(): jnp.einsum('ijab,jkbc->ikac', kept, column_both, preferred_element_type=j...  15.1 us
    unnamed x27, local copies, waits for them, and re-layouts  10 us
  transfers between devices with their start and end apart: 3, of which 3 were waited for; matrix products, arithmetic and copies ran while one was open for 1% of the time, Pallas kernels for 0%

commit v1 on v0

--- a/solution.py
+++ b/solution.py
@@ -6,7 +6,7 @@
 
 def from_root(block, axis, owner):
     block = jnp.where(lax.axis_index(axis) == owner, block, jnp.zeros_like(block))
-    return lax.psum(block, axis)
+    return jnp.sum(lax.all_gather(block, axis), axis=0)
 
 
 def shards(

time: 413 us -> 446 us (1.080)
  waiting for transfers between devices: 353 us -> 380 us
  other arithmetic: 7.64 us -> 19.8 us
    all_gather x0 -> x2, waiting for transfers between devices: none -> 95.6 us  [from_root(): return jnp.sum(lax.all_gather(block, axis), axis=0)]
    psum x1 -> x0, waiting for transfers between devices: 67.1 us -> none  [from_root(): return lax.psum(block, axis)]
    reduce_sum x0 -> x2, other arithmetic: none -> 10 us  [from_root(): return jnp.sum(lax.all_gather(block, axis), axis=0)]
    unnamed x27 -> x23, local copies, waits for them, and re-layouts: 10 us -> 3.41 us
    unnamed x4 -> x5, waiting for transfers between devices: 140 us -> 137 us
  transfers between devices with their start and end apart: 3 -> 4, of which waited for: 3 -> 4; matrix products, arithmetic and copies ran while one was open for 1% -> 3% of each run, Pallas kernels for 0% -> 0%
where the time goes in v1:
time: 446 us; the launch traced here: 445 us
  waiting for transfers between devices  380 us (85%)
  matrix products  23.1 us (5%)
  other arithmetic  19.8 us (4%)
  between operations  15.3 us (3%)
  local copies, waits for them, and re-layouts  7.28 us (2%)
    psum x1, waiting for transfers between devices, shards(): lax.psum((part_one, v_part, part_two), ('row', 'col'))  146 us
    unnamed x5, waiting for transfers between devices  137 us
    all_gather x2, waiting for transfers between devices, from_root(): return jnp.sum(lax.all_gather(block, axis), axis=0)  95.6 us
    dot_general x1, matrix products, shards(): jnp.einsum('ijab,jkbc->ikac', kept, column_both, preferred_element_type=j...  15.1 us
    reduce_sum x2, other arithmetic, from_root(): return jnp.sum(lax.all_gather(block, axis), axis=0)  10 us
  transfers between devices with their start and end apart: 4, of which 4 were waited for; matrix products, arithmetic and copies ran while one was open for 3% of the time, Pallas kernels for 0%

profile of v1, /device:TPU:1, one launch (start us, length us, event | category | flops | bytes accessed | tf_op | source)
XLA Modules:
  0.0 445.1 jit_solution(619192011388503432)
XLA Ops:
  7.3 0.8 dynamic-slice_compare_fusion
  8.0 1.8 broadcast_select_fusion.1
  9.8 1.3 copy-done.1
  11.2 1.1 dynamic-slice_select_fusion.1
  12.3 1.8 broadcast_select_fusion
  14.1 1.1 dynamic-slice_select_fusion
  15.3 50.3 %all-gather.5.cloned.1.call-done = bf16[64,256,256]{2,1,0:T(8,128)(2,1)} async-done(((bf16[8,256,256]{2,1,0:T(8,128)(2,1)}), bf16[64,256,256]{2,1,0:T(8,128)(2,1)}) %all-gather.5.cloned.1.call-update) | async-done | bytes 8388624 | tf_op jit(solution)/shard_map/all_gather | solution.py:9
  65.7 5.0 %reduce_sum.24 = bf16[8,256,256]{2,1,0:T(8,128)(2,1)S(1)} reduce(bf16[8,8,256,256]{3,2,1,0:T(8,128)(2,1)} %bitcast.63, bf16[]{:T(256)} %constant.45.clone.1), dimensions={0}, to_apply=%region_0.1 | reduce | flops 3670016 | bytes 9437186 | tf_op jit(solution)/shard_map/reduce_sum | solution.py:9
  70.7 1.3 copy.19
  72.0 45.3 %all-gather.7.cloned.1.call-done = bf16[64,256,256]{2,1,0:T(8,128)(2,1)} async-done(((bf16[8,256,256]{2,1,0:T(8,128)(2,1)}), bf16[64,256,256]{2,1,0:T(8,128)(2,1)}) %all-gather.7.cloned.1.call-update) | async-done | bytes 8388624 | tf_op jit(solution)/shard_map/all_gather | solution.py:9
  117.2 5.0 %reduce_sum.25 = bf16[8,256,256]{2,1,0:T(8,128)(2,1)S(1)} reduce(bf16[8,8,256,256]{3,2,1,0:T(8,128)(2,1)} %bitcast.64, bf16[]{:T(256)} %constant.45.clone.1), dimensions={0}, to_apply=%region_1.2 | reduce | flops 3670016 | bytes 9437186 | tf_op jit(solution)/shard_map/reduce_sum | solution.py:9
  122.3 1.3 copy.20
  123.6 15.1 %fusion.5 = f32[16,2,256,256]{2,3,0,1:T(8,128)} fusion(bf16[16,8,256,256]{3,2,1,0:T(8,128)(2,1)} %param.9, pred[16,8]{1,0:T(8,128)(4,1)S(1)} %copy.21, bf16[8,1,256,256]{2,3,0,1:T(8,128)(2,1)} %bitcast.67, bf16[8,1,256,256]{2,3,0,1:T(8,128)(2,1)} %bitcast.66), kind=kOutput, calls=%fused_computation.5 | convolution fusion | flops 8602517504 | bytes 27263104 | tf_op jit(solution)/shard_map/ijab,jkbc->ikac/dot_general | solution.py:48
  142.4 137.4 %all-reduce.5.cloned.1.call-done = f32[16,2,256,256]{2,3,0,1:T(8,128)} async-done(((f32[16,2,256,256]{2,3,0,1:T(8,128)}), f32[16,2,256,256]{2,3,0,1:T(8,128)}) %all-reduce.5.cloned.1.call-update) | async-done | bytes 8388624
  279.8 1.7 constant_dynamic-slice_fusion
  281.7 0.9 fusion.20
  282.8 1.1 fusion.18
  283.9 2.7 fusion.15
  286.6 0.8 copy.24
  287.4 0.7 fusion.17
  288.1 146.4 %all-reduce.7.cloned.1.call-done = (f32[256,256]{1,0:T(8,128)}, f32[256,256]{1,0:T(8,128)}, f32[256,256]{1,0:T(8,128)}) async-done(((f32[256,256]{1,0:T(8,128)}, f32[256,256]{1,0:T(8,128)}, f32[256,256]{1,0:T(8,128)}), (f32[256,256]{1,0:T(8,128)}, f32[256,256]{1,0:T(8,128)}, f32[256,256]{1,0:T(8,128)})) %all-reduce.7.cloned.1.call-update) | async-done | bytes 786448 | tf_op jit(solution)/shard_map/psum | solution.py:72
  434.5 1.0 add_convert_fusion
  435.5 1.2 fusion.14
  436.7 1.9 fusion.13
  (34 shorter events, 3.0 us)
Async XLA Ops:
  7.2 275.4 %copy-start = (bf16[256,256]{1,0:T(8,128)(2,1)S(1)}, bf16[256,256]{1,0:T(8,128)(2,1)}, u32[]{:S(2)}) copy-start(bf16[256,256]{1,0:T(8,128)(2,1)} %param.15) | copy-start | bytes 393220
  7.2 58.5 %all-gather.5.cloned.1.call-start = ((), (), s32[]{:S(2)}) async-start(), calls=%async_computation | async-start | bytes 9437184 | tf_op jit(solution)/shard_map/all_gather | solution.py:9
  9.8 1.3 copy-start.1
  12.2 105.0 %all-gather.7.cloned.1.call-start = ((), (), s32[]{:S(2)}) async-start(), calls=%async_computation.1 | async-start | bytes 9437184 | tf_op jit(solution)/shard_map/all_gather | solution.py:9
  14.1 1.1 copy-start.6
  15.2 264.6 %all-reduce.5.cloned.1.call-start = ((), (), s32[]{:S(2)}) async-start(), calls=%async_computation.2 | async-start | bytes 16777216
  138.6 0.7 copy-start.7
  138.6 1.2 copy-start.8
  138.7 3.1 copy-start.9
  138.7 295.8 %all-reduce.7.cloned.1.call-start = ((), (), s32[]{:S(2)}) async-start(), calls=%async_computation.3 | async-start | bytes 1572864 | tf_op jit(solution)/shard_map/psum | solution.py:72
  281.6 152.9 %copy-start.5 = (f32[256,256]{1,0:T(8,128)S(1)}, f32[256,256]{1,0:T(8,128)}, u32[]{:S(2)}) copy-start(f32[256,256]{1,0:T(8,128)} %param.16) | copy-start | bytes 786436
  282.8 153.9 %copy-start.4 = (f32[256,256]{1,0:T(8,128)S(1)}, f32[256,256]{1,0:T(8,128)}, u32[]{:S(2)}) copy-start(f32[256,256]{1,0:T(8,128)} %param.17) | copy-start | bytes 786436
  435.5 3.1 copy-start.2
  436.7 1.9 copy-start.3
Sparse Core Ops, SparseCore 0:
  12.4 53.2 all-gather.4
  67.4 49.8 all-gather.6
  138.8 140.9 all-reduce.4
  286.7 147.7 all-reduce.6
